TPU v7x, 256 devices: a whole 4x4x8 slice. The times are simulated.
256 devices in a mesh: session: 8 (over x_lo, y), ctx: 32 (over x_hi, z, core).
Axes of the slice: x: 4 (x_hi: 2, x_lo: 2; x = x_hi * 2 + x_lo), y: 4, z: 8, core: 2. Of those that a mesh axis runs over, the one named last changes fastest.
Arguments:
- frames: float32 [49152, 1024], P(('session', 'ctx')), parts along dimension 0, may hold values from -6 to 6
- attend_gain: float32 [1024], replicated, may hold values from 0.25 to 1.75
- query_weight: bfloat16 [1024, 1024], replicated, may hold values from -8 to 8
- key_weight: bfloat16 [1024, 1024], replicated, may hold values from -8 to 8
- value_weight: bfloat16 [1024, 1024], replicated, may hold values from -0.1875 to 0.1875
- output_weight: bfloat16 [1024, 1024], replicated, may hold values from -0.1875 to 0.1875
- mixer_gain: float32 [1024], replicated, may hold values from 0.25 to 1.75
- depthwise: float32 [31, 1024], replicated, may hold values from -1 to 1
- mixer_bias: float32 [1024], replicated, may hold values from -3 to 3
Outputs:
- block_out: float32 [49152, 1024], P(('session', 'ctx')), parts along dimension 0
There are 8 independent parts, one for each index of `session`. A program takes and returns all parts, laid end to end along the dimension named above; an argument that names none is the same for every part. Nothing has to cross between parts.
All inputs are finite; a program needn't handle non-finite values.
Results may differ from a plain program's by a relative error of at most 0.0031.
Values may be sent and summed in bfloat16 or wider, within the bound.
A program may use at most 256 MiB of HBM per device.

v0:
```python
import jax
import jax.numpy as jnp
from jax import lax
from jax.sharding import PartitionSpec as P

HEADS = 16
KERNEL = 31


def with_halo(block, sides, width):
    for axis, dim in sides:
        count = lax.axis_size(axis)
        forward = [(i, i + 1) for i in range(count - 1)]
        backward = [(target, source) for source, target in forward]
        low = lax.ppermute(
            lax.slice_in_dim(block, block.shape[dim] - width, None, axis=dim), axis, forward
        )
        high = lax.ppermute(lax.slice_in_dim(block, 0, width, axis=dim), axis, backward)
        block = jnp.concatenate([low, block, high], axis=dim)
    return block


def norm_rows(values_in, gain):
    center = jnp.mean(values_in, axis=1, keepdims=True)
    spread = jnp.mean(jnp.square(values_in - center), axis=1, keepdims=True)
    return (values_in - center) * lax.rsqrt(spread + 1e-05) * gain


def project(source, weight):
    return jnp.dot(source, weight, preferred_element_type=jnp.float32).astype(jnp.bfloat16)


def per_device(
    frames,
    attend_gain,
    query_weight,
    key_weight,
    value_weight,
    output_weight,
    mixer_gain,
    depthwise,
    mixer_bias,
):
    row_count, feature_count = frames.shape
    head_size = feature_count // HEADS
    score_scale = head_size ** (-0.5)
    normed = norm_rows(frames, attend_gain).astype(jnp.bfloat16)
    query_heads = project(normed, query_weight).reshape(row_count, HEADS, head_size)
    key_rows = project(normed, key_weight)
    value_rows = project(normed, value_weight)
    key_block = lax.all_gather(key_rows, "ctx", axis=0, tiled=True)
    highest = jnp.full((HEADS, row_count), -1e30, jnp.float32)
    block_rows = key_block.shape[0]
    key_heads = key_block.reshape(block_rows, HEADS, head_size)
    value_heads = lax.all_gather(value_rows, "ctx", axis=0, tiled=True).reshape(
        block_rows, HEADS, head_size
    )
    scores = (
        jnp.einsum("qhd,khd->hqk", query_heads, key_heads, preferred_element_type=jnp.float32)
        * score_scale
    )
    new_high = jnp.maximum(highest, jnp.max(scores, axis=2))
    weights = jnp.exp(scores - new_high[:, :, None])
    partial_sum = jnp.einsum(
        "hqk,khd->qhd",
        weights.astype(jnp.bfloat16),
        value_heads,
        preferred_element_type=jnp.float32,
    )
    totals = jnp.sum(weights, axis=2)
    running = partial_sum
    highest, totals, running = (new_high, totals, running)
    context = (
        (running / jnp.transpose(totals)[:, :, None])
        .reshape(row_count, feature_count)
        .astype(jnp.bfloat16)
    )
    attended = frames + jnp.dot(context, output_weight, preferred_element_type=jnp.float32)
    mixer_in = norm_rows(attended, mixer_gain)
    half_width = KERNEL // 2
    padded = with_halo(mixer_in, (("ctx", 0),), half_width)
    convolved = jnp.zeros_like(mixer_in) + mixer_bias
    for tap_index in range(KERNEL):
        convolved = convolved + padded[tap_index : tap_index + row_count] * depthwise[tap_index]
    return attended + jax.nn.silu(convolved)


def solution(mesh):
    in_specs = (P(("session", "ctx"), None), P(), P(), P(), P(), P(), P(), P(), P())
    out_specs = P(("session", "ctx"), None)
    return jax.shard_map(
        per_device, mesh=mesh, in_specs=in_specs, out_specs=out_specs, check_vma=False
    )
```

profile of v0, /device:TPU:1, one launch (start us, length us, event | category | flops | bytes accessed | tf_op | source)
XLA Modules:
  0.0 318.0 jit_solution(9778761787293347411)
XLA Ops:
  6.5 0.0 copy-start
  6.5 0.0 copy-start.2
  6.5 0.0 all-gather.5.cloned.1.call-start
  6.5 1.4 reduce_sum.45
  8.0 1.4 multiply_reduce_fusion.2
  9.3 3.3 %convolution_convert_fusion = bf16[192,1024]{1,0:T(8,128)(2,1)} fusion(bf16[1024,1024]{1,0:T(8,128)(2,1)} %param.12, f32[192,1024]{1,0:T(8,128)} %param.9, f32[1024]{0:T(1024)} %param.10, f32[192]{0:T(256)S(1)} %add_rsqrt_fusion.1, f32[192]{0:T(256)S(1)} %broadcast_multiply_fusion.1), kind=kOutput, calls=%fused_computation.37 | convolution fusion | flops 403636224 | bytes 3282432 | tf_op jit(solution)/shard_map/dot_general | solution.py:30
  12.6 0.0 all-gather.5.cloned.1.call-update
  12.6 0.0 all-gather.3.cloned.1.call-start
  12.7 3.2 %convolution_convert_fusion.2 = bf16[192,1024]{1,0:T(8,128)(2,1)} fusion(bf16[1024,1024]{1,0:T(8,128)(2,1)} %param.13, f32[192,1024]{1,0:T(8,128)} %param.9, f32[1024]{0:T(1024)} %param.10, f32[192]{0:T(256)S(1)} %add_rsqrt_fusion.1, f32[192]{0:T(256)S(1)} %broadcast_multiply_fusion.1), kind=kOutput, calls=%fused_computation.39 | convolution fusion | flops 403636224 | bytes 3282432 | tf_op jit(solution)/shard_map/dot_general | solution.py:30
  15.9 0.0 all-gather.3.cloned.1.call-update
  15.9 2.5 convolution_convert_fusion.1
  18.4 0.2 copy.14
  18.6 0.0 copy-done.2
  18.7 0.1 fusion.106
  18.7 115.4 %all-gather.5.cloned.1.call-done = bf16[6144,1024]{1,0:T(8,128)(2,1)} async-done(((bf16[192,1024]{1,0:T(8,128)(2,1)}), bf16[6144,1024]{1,0:T(8,128)(2,1)}) %all-gather.5.cloned.1.call-update) | async-done | bytes 12582928 | tf_op jit(solution)/shard_map/all_gather | solution.py:51
  134.1 16.7 %copy.15 = bf16[6144,1024]{0,1:T(8,128)(2,1)} copy(bf16[6144,1024]{1,0:T(8,128)(2,1)} %all-gather.5.cloned.1.call-done) | data formatting | bytes 25165824 | tf_op jit(solution)/shard_map/all_gather | solution.py:51
  150.8 30.4 %multiply_reduce_fusion = (f32[16,192]{1,0:T(8,128)S(1)}, f32[16,192,6144]{2,1,0:T(8,128)}) fusion(bf16[192,16,64]{0,2,1:T(8,128)(2,1)S(1)} %bitcast.53, bf16[6144,16,64]{0,2,1:T(8,128)(2,1)} %bitcast.50), kind=kOutput, calls=%fused_computation.1 | convolution fusion | flops 2453664768 | bytes 88485888 | tf_op jit(solution)/shard_map/qhd,khd->hqk/dot_general | solution.py:59
  181.2 25.1 %fusion = f32[16,192]{1,0:T(8,128)S(1)} fusion(f32[16,192,6144]{2,1,0:T(8,128)} %get-tuple-element.39, f32[16,192]{1,0:T(8,128)S(1)} %broadcast_maximum_fusion), kind=kLoop, calls=%fused_computation.2 | loop fusion | flops 56620032 | bytes 75522048 | tf_op jit(solution)/shard_map/reduce_sum | solution.py:70
  206.3 44.6 %all-gather.3.cloned.1.call-done = bf16[6144,1024]{1,0:T(8,128)(2,1)} async-done(((bf16[192,1024]{1,0:T(8,128)(2,1)}), bf16[6144,1024]{1,0:T(8,128)(2,1)}) %all-gather.3.cloned.1.call-update) | async-done | bytes 12582928 | tf_op jit(solution)/shard_map/all_gather | solution.py:55
  250.8 16.7 %copy.13 = bf16[6144,1024]{0,1:T(8,128)(2,1)} copy(bf16[6144,1024]{1,0:T(8,128)(2,1)} %all-gather.3.cloned.1.call-done) | data formatting | bytes 25165824 | tf_op jit(solution)/shard_map/all_gather | solution.py:55
  267.5 0.0 copy-start.1
  267.6 0.0 copy-start.3
  267.6 0.0 copy-start.4
  267.6 29.8 %fusion.12 = bf16[192,16,64]{0,2,1:T(8,128)(2,1)S(1)} fusion(bf16[6144,16,64]{0,2,1:T(8,128)(2,1)} %bitcast.51, f32[16,192,6144]{2,1,0:T(8,128)} %get-tuple-element.39, f32[16,192]{1,0:T(8,128)S(1)} %broadcast_maximum_fusion, f32[192,16]{0,1:T(8,128)S(1)} %bitcast.54), kind=kOutput, calls=%fused_computation.41 | convolution fusion | flops 2472935424 | bytes 88498176 | tf_op jit(solution)/shard_map/hqk,khd->qhd/dot_general | solution.py:64
  297.3 0.0 copy-done
  297.4 0.0 copy-done.1
  297.4 0.7 fusion.108
  298.1 0.2 multiply_reduce_fusion.1
  298.3 0.0 copy-done.3
  298.3 0.2 multiply_multiply_fusion
  298.5 2.7 collective-permute-start
  301.2 1.9 collective-permute-start.1
  303.1 1.1 fusion.107
  304.3 0.0 collective-permute-done
  304.3 2.5 collective-permute-done.1
  306.8 0.0 copy-done.4
  306.8 4.4 %multiply_add_fusion = f32[192,1024]{1,0:T(8,128)} fusion(f32[192,1024]{1,0:T(8,128)S(1)} %get-tuple-element.41, f32[15,1024]{1,0:T(8,128)S(1)} %collective-permute-done.1, f32[192,1024]{1,0:T(8,128)S(1)} %multiply_multiply_fusion, f32[15,1024]{1,0:T(8,128)S(1)} %collective-permute-done, f32[1024]{0:T(1024)S(1)} %bitcast.84, f32[1024]{0:T(1024)S(1)} %bitcast.85, ...), kind=kLoop, calls=%fused_computation.157 | loop fusion | flops 19070976 | bytes 2613248 | tf_op jit(solution)/shard_map/add | solution.py:85
  (6 shorter events, 0.0 us)
Async XLA Ops:
  6.5 290.8 %copy-start = (bf16[1024,1024]{1,0:T(8,128)(2,1)S(1)}, bf16[1024,1024]{1,0:T(8,128)(2,1)}, u32[]{:S(2)}) copy-start(bf16[1024,1024]{1,0:T(8,128)(2,1)} %param.14) | copy-start | bytes 6291460
  6.5 12.1 %copy-start.2 = (f32[31,1024]{1,0:T(8,128)S(1)}, f32[31,1024]{1,0:T(8,128)}, u32[]{:S(2)}) copy-start(f32[31,1024]{1,0:T(8,128)} %param.16) | copy-start | bytes 380932
  6.5 127.5 %all-gather.5.cloned.1.call-start = ((), (), s32[]{:S(2)}) async-start(), calls=%async_computation.1 | async-start | bytes 12976128 | tf_op jit(solution)/shard_map/all_gather | solution.py:51
  12.6 238.2 %all-gather.3.cloned.1.call-start = ((), (), s32[]{:S(2)}) async-start(), calls=%async_computation | async-start | bytes 12976128 | tf_op jit(solution)/shard_map/all_gather | solution.py:55
  267.5 29.8 %copy-start.1 = (f32[192,1024]{1,0:T(8,128)S(1)}, f32[192,1024]{1,0:T(8,128)}, u32[]{:S(2)}) copy-start(f32[192,1024]{1,0:T(8,128)} %param.9) | copy-start | bytes 2359300
  267.6 30.8 %copy-start.3 = (f32[1024]{0:T(1024)S(1)}, f32[1024]{0:T(1024)}, u32[]{:S(2)}) copy-start(f32[1024]{0:T(1024)} %param.15) | copy-start | bytes 12292
  267.6 39.2 %copy-start.4 = (f32[1024]{0:T(1024)S(1)}, f32[1024]{0:T(1024)}, u32[]{:S(2)}) copy-start(f32[1024]{0:T(1024)} %param.17) | copy-start | bytes 12292
  298.5 5.7 %collective-permute-start = (f32[15,1024]{1,0:T(8,128)S(1)}, f32[15,1024]{1,0:T(8,128)S(1)}, u32[]{:S(2)}, u32[]{:S(2)}) collective-permute-start(f32[15,1024]{1,0:T(8,128)S(1)} %get-tuple-element.5), channel_id=1, source_target_pairs={{0,1},{1,2},{2,3},{3,4},{4,5},{5,6},{6,7},{7,8},{8,9},{9,10},{10,1... | collective-permute-start | bytes 184328 | tf_op jit(solution)/shard_map/ppermute | solution.py:15
  301.2 5.6 %collective-permute-start.1 = (f32[15,1024]{1,0:T(8,128)S(1)}, f32[15,1024]{1,0:T(8,128)S(1)}, u32[]{:S(2)}, u32[]{:S(2)}) collective-permute-start(f32[15,1024]{1,0:T(8,128)S(1)} %get-tuple-element.6), channel_id=1, source_target_pairs={{1,0},{2,1},{3,2},{4,3},{5,4},{6,5},{7,6},{8,7},{9,8},{10,9},{11,1... | collective-permute-start | bytes 184328 | tf_op jit(solution)/shard_map/ppermute | solution.py:18
Sparse Core Ops, SparseCore 0:
  12.7 121.2 all-gather.4
  136.8 113.9 all-gather.2
where the time goes:
time: 319 us; the launch traced here: 318 us
  waiting for transfers between devices  162 us (51%)
  matrix products  69.8 us (22%)
  local copies, waits for them, and re-layouts  34.9 us (11%)
  other arithmetic  32.7 us (10%)
  between operations  13.5 us (4%)
  starting transfers between devices  4.63 us (1%)
    all_gather x1, waiting for transfers between devices, per_device(): key_block = lax.all_gather(key_rows, 'ctx', axis=0, tiled=True)  115 us
    all_gather x1, waiting for transfers between devices, per_device(): lax.all_gather(value_rows, 'ctx', axis=0, tiled=True)  44.6 us
    dot_general x1, matrix products, per_device(): jnp.einsum('qhd,khd->hqk', query_heads, key_heads, preferred_element_type...  30.4 us
    dot_general x1, matrix products, per_device(): jnp.einsum('hqk,khd->qhd', weights.astype(jnp.bfloat16), value_heads, pre...  29.8 us
    reduce_sum x1, other arithmetic, per_device(): totals = jnp.sum(weights, axis=2)  25.1 us
    all_gather x1, local copies, waits for them, and re-layouts, per_device(): key_block = lax.all_gather(key_rows, 'ctx', axis=0, tiled=True)  16.7 us
    all_gather x1, local copies, waits for them, and re-layouts, per_device(): lax.all_gather(value_rows, 'ctx', axis=0, tiled=True)  16.7 us
    dot_general x3, matrix products, project(): jnp.dot(source, weight, preferred_element_type=jnp.float32)  8.98 us
  transfers between devices with their start and end apart: 4, of which 3 were waited for; matrix products, arithmetic and copies ran while one was open for 25% of the time, Pallas kernels for 0%

commit v1 on v0

--- a/solution.py
+++ b/solution.py
@@ -52,9 +52,9 @@
     highest = jnp.full((HEADS, row_count), -1e30, jnp.float32)
     block_rows = key_block.shape[0]
     key_heads = key_block.reshape(block_rows, HEADS, head_size)
-    value_heads = lax.all_gather(value_rows, "ctx", axis=0, tiled=True).reshape(
-        block_rows, HEADS, head_size
-    )
+    value_heads = jnp.concatenate(
+        lax.all_to_all(jnp.stack([value_rows] * lax.axis_size("ctx")), "ctx", 0, 0), axis=0
+    ).reshape(block_rows, HEADS, head_size)
     scores = (
         jnp.einsum("qhd,khd->hqk", query_heads, key_heads, preferred_element_type=jnp.float32)
         * score_scale

time: 319 us -> 530 us (1.66); the launches traced: 318 us -> 523 us
  waiting for transfers between devices: 162 us -> 311 us
  local copies, waits for them, and re-layouts: 34.9 us -> 76.6 us
  starting transfers between devices: 4.63 us -> 20.5 us
    all_to_all x0 -> x1, waiting for transfers between devices: none -> 311 us  [per_device(): lax.all_to_all(jnp.stack([value_rows] * lax.axis_size('ctx')), 'ctx', 0, 0)]
    all_gather x1, waiting for transfers between devices: 115 us -> 0.01 us  [per_device(): key_block = lax.all_gather(key_rows, 'ctx', axis=0, tiled=True)]
    all_gather x1 -> x0, waiting for transfers between devices: 44.6 us -> none  [per_device(): lax.all_gather(value_rows, 'ctx', axis=0, tiled=True)]
    another operation x0 -> x2, local copies, waits for them, and re-layouts: none -> 32.6 us  [the longest x1 26.4 us: per_device(): value_heads = jnp.concatenate(lax.all_to_all(jnp.stack([value_rows] * lax...]
    all_to_all x0 -> x1, local copies, waits for them, and re-layouts: none -> 24.3 us  [per_device(): lax.all_to_all(jnp.stack([value_rows] * lax.axis_size('ctx')), 'ctx', 0, 0)]
    all_gather x1 -> x0, local copies, waits for them, and re-layouts: 16.7 us -> none  [per_device(): lax.all_gather(value_rows, 'ctx', axis=0, tiled=True)]
    all_to_all x0 -> x1, starting transfers between devices: none -> 12.7 us  [per_device(): lax.all_to_all(jnp.stack([value_rows] * lax.axis_size('ctx')), 'ctx', 0, 0)]
  transfers between devices with their start and end apart: 4 -> 4, of which waited for: 3 -> 2; matrix products, arithmetic and copies ran while one was open for 25% -> 11% of each run, Pallas kernels for 0% -> 0%
where the time goes in v1:
time: 530 us; the launch traced here: 523 us
  waiting for transfers between devices  311 us (59%)
  local copies, waits for them, and re-layouts  76.6 us (14%)
  matrix products  68.9 us (13%)
  other arithmetic  32.1 us (6%)
  starting transfers between devices  20.5 us (4%)
  between operations  13.8 us (3%)
    all_to_all x1, waiting for transfers between devices, per_device(): lax.all_to_all(jnp.stack([value_rows] * lax.axis_size('ctx')), 'ctx', 0, 0)  311 us
    dot_general x1, matrix products, per_device(): jnp.einsum('qhd,khd->hqk', query_heads, key_heads, preferred_element_type...  30.1 us
    dot_general x1, matrix products, per_device(): jnp.einsum('hqk,khd->qhd', weights.astype(jnp.bfloat16), value_heads, pre...  29.6 us
    another operation x1, local copies, waits for them, and re-layouts, per_device(): value_heads = jnp.concatenate(lax.all_to_all(jnp.stack([value_rows] * lax...  26.4 us
    all_to_all x1, local copies, waits for them, and re-layouts, per_device(): lax.all_to_all(jnp.stack([value_rows] * lax.axis_size('ctx')), 'ctx', 0, 0)  24.3 us
    reduce_sum x1, other arithmetic, per_device(): totals = jnp.sum(weights, axis=2)  23.7 us
    all_gather x1, local copies, waits for them, and re-layouts, per_device(): key_block = lax.all_gather(key_rows, 'ctx', axis=0, tiled=True)  16.6 us
    all_to_all x1, starting transfers between devices, per_device(): lax.all_to_all(jnp.stack([value_rows] * lax.axis_size('ctx')), 'ctx', 0, 0)  12.7 us
  transfers between devices with their start and end apart: 4, of which 2 were waited for; matrix products, arithmetic and copies ran while one was open for 11% of the time, Pallas kernels for 0%

profile of v1, /device:TPU:1, one launch (start us, length us, event | category | flops | bytes accessed | tf_op | source)
XLA Modules:
  0.0 523.1 jit_solution(11825695588372493403)
XLA Ops:
  6.5 0.0 copy-start
  6.5 1.4 reduce_sum.45
  8.0 1.4 multiply_reduce_fusion.2
  9.3 2.5 convolution_convert_fusion.2
  11.8 6.1 %stack.2 = bf16[32,192,1024]{2,1,0:T(8,128)(2,1)} broadcast(bf16[192,1024]{1,0:T(8,128)(2,1)S(1)} %convolution_convert_fusion.2), dimensions={1,2} | broadcast | bytes 12976128 | tf_op jit(solution)/shard_map/stack | solution.py:56
  18.0 12.7 %all-to-all-start = ((bf16[32,192,1024]{2,1,0:T(8,128)(2,1)}), bf16[32,192,1024]{2,1,0:T(8,128)(2,1)}, u32[]{:S(2)}, u32[]{:S(2)}) async-start(bf16[32,192,1024]{2,1,0:T(8,128)(2,1)} %stack.2), calls=%async_computation | async-start | bytes 25165824 | tf_op jit(solution)/shard_map/all_to_all | solution.py:56
  30.7 0.0 all-gather.2.cloned.1.call-start
  30.8 0.0 copy-done.1
  30.8 0.0 copy-done.3
  30.8 3.0 convolution_convert_fusion
  33.8 0.0 all-gather.2.cloned.1.call-update
  33.8 3.0 convolution_convert_fusion.1
  36.8 1.2 copy.17
  38.0 0.0 copy-done.2
  38.0 0.7 fusion.106
  38.7 311.1 %all-to-all-done = bf16[32,192,1024]{2,1,0:T(8,128)(2,1)} async-done(((bf16[32,192,1024]{2,1,0:T(8,128)(2,1)}), bf16[32,192,1024]{2,1,0:T(8,128)(2,1)}, u32[]{:S(2)}, u32[]{:S(2)}) %all-to-all-start) | async-done | bytes 12582944 | tf_op jit(solution)/shard_map/all_to_all | solution.py:56
  349.8 24.3 %copy.16 = bf16[32,192,1024]{1,0,2:T(8,128)(2,1)} copy(bf16[32,192,1024]{2,1,0:T(8,128)(2,1)} %all-to-all-done) | data formatting | bytes 25165824 | tf_op jit(solution)/shard_map/all_to_all | solution.py:56
  374.1 26.4 %reshape_reshape.3 = bf16[6144,16,64]{0,2,1:T(8,128)(2,1)} reshape(bf16[32,192,1024]{1,0,2:T(8,128)(2,1)} %copy.16) | data formatting | bytes 25165824 | tf_op jit(solution)/shard_map/reshape;reshape | solution.py:57
  400.5 16.6 %copy.18 = bf16[6144,1024]{0,1:T(8,128)(2,1)} copy(bf16[6144,1024]{1,0:T(8,128)(2,1)} %all-gather.2.cloned.1.call-done) | data formatting | bytes 25165824 | tf_op jit(solution)/shard_map/all_gather | solution.py:51
  417.2 30.1 %multiply_reduce_fusion = (f32[16,192]{1,0:T(8,128)S(1)}, f32[16,192,6144]{2,1,0:T(8,128)}) fusion(bf16[192,16,64]{0,2,1:T(8,128)(2,1)S(1)} %bitcast.53, bf16[6144,16,64]{0,2,1:T(8,128)(2,1)} %bitcast.51), kind=kOutput, calls=%fused_computation.1 | convolution fusion | flops 2453664768 | bytes 88485888 | tf_op jit(solution)/shard_map/qhd,khd->hqk/dot_general | solution.py:59
  447.3 23.7 %fusion = f32[16,192]{1,0:T(8,128)S(1)} fusion(f32[16,192,6144]{2,1,0:T(8,128)} %get-tuple-element.39, f32[16,192]{1,0:T(8,128)S(1)} %broadcast_maximum_fusion), kind=kLoop, calls=%fused_computation.2 | loop fusion | flops 56620032 | bytes 75522048 | tf_op jit(solution)/shard_map/reduce_sum | solution.py:70
  471.0 0.0 copy-start.19
  471.1 0.0 copy-start.4
  471.1 0.0 copy-start.5
  471.1 0.0 copy-start.6
  471.1 0.0 copy-start.7
  471.1 0.0 copy-start.8
  471.1 0.0 copy-start.9
  471.1 0.0 copy-start.10
  471.1 0.0 copy-start.11
  471.1 0.0 copy-start.12
  471.1 0.0 copy-start.13
  471.2 0.0 copy-start.14
  471.2 0.0 copy-start.15
  471.2 0.0 copy-start.16
  471.2 0.0 copy-start.17
  471.2 29.6 %fusion.12 = bf16[192,16,64]{0,2,1:T(8,128)(2,1)S(1)} fusion(bf16[6144,16,64]{0,2,1:T(8,128)(2,1)} %reshape_reshape.3, f32[16,192,6144]{2,1,0:T(8,128)} %get-tuple-element.39, f32[16,192]{1,0:T(8,128)S(1)} %broadcast_maximum_fusion, f32[192,16]{0,1:T(8,128)S(1)} %bitcast.54), kind=kOutput, calls=%fused_computation.41 | convolution fusion | flops 2472935424 | bytes 88498176 | tf_op jit(solution)/shard_map/hqk,khd->qhd/dot_general | solution.py:64
  500.8 0.0 copy-done
  500.8 0.7 fusion.108
  501.5 0.2 multiply_reduce_fusion.1
  501.8 0.2 multiply_multiply_fusion
  502.0 5.7 %collective-permute-start.1 = (f32[15,1024]{1,0:T(8,128)S(1)}, f32[15,1024]{1,0:T(8,128)S(1)}, u32[]{:S(2)}, u32[]{:S(2)}) collective-permute-start(f32[15,1024]{1,0:T(8,128)S(1)} %get-tuple-element.6), channel_id=1, source_target_pairs={{1,0},{2,1},{3,2},{4,3},{5,4},{6,5},{7,6},{8,7},{9,8},{10,9},{11,1... | collective-permute-start | bytes 184328 | tf_op jit(solution)/shard_map/ppermute | solution.py:18
  507.7 1.9 collective-permute-start
  509.6 1.1 fusion.107
  510.8 0.0 collective-permute-done.1
  510.8 0.2 collective-permute-done
  511.0 0.0 copy-done.5
  511.1 5.2 multiply_add_fusion
  (26 shorter events, 0.1 us)
Async XLA Ops:
  6.5 494.2 %copy-start = (bf16[1024,1024]{1,0:T(8,128)(2,1)S(1)}, bf16[1024,1024]{1,0:T(8,128)(2,1)}, u32[]{:S(2)}) copy-start(bf16[1024,1024]{1,0:T(8,128)(2,1)} %param.14) | copy-start | bytes 6291460
  18.0 12.8 %copy-start.1 = (f32[192,1024]{1,0:T(8,128)S(1)}, f32[192,1024]{1,0:T(8,128)}, u32[]{:S(2)}) copy-start(f32[192,1024]{1,0:T(8,128)} %param.9) | copy-start | bytes 2359300
  18.0 12.8 %copy-start.3 = (f32[1024]{0:T(1024)S(1)}, f32[1024]{0:T(1024)}, u32[]{:S(2)}) copy-start(f32[1024]{0:T(1024)} %param.10) | copy-start | bytes 12292
  18.0 20.0 %copy-start.2 = (f32[31,1024]{1,0:T(8,128)S(1)}, f32[31,1024]{1,0:T(8,128)}, u32[]{:S(2)}) copy-start(f32[31,1024]{1,0:T(8,128)} %param.16) | copy-start | bytes 380932
  18.0 331.8 %all-to-all-start = ((bf16[32,192,1024]{2,1,0:T(8,128)(2,1)}), bf16[32,192,1024]{2,1,0:T(8,128)(2,1)}, u32[]{:S(2)}, u32[]{:S(2)}) async-start(bf16[32,192,1024]{2,1,0:T(8,128)(2,1)} %stack.2), calls=%async_computation | async-start | bytes 25165824 | tf_op jit(solution)/shard_map/all_to_all | solution.py:56
  30.7 369.8 %all-gather.2.cloned.1.call-start = ((), (), s32[]{:S(2)}) async-start(), calls=%async_computation.1 | async-start | bytes 12976128 | tf_op jit(solution)/shard_map/all_gather | solution.py:51
  471.0 30.7 %copy-start.19 = (f32[1024]{0:T(1024)S(1)}, f32[1024]{0:T(1024)}, u32[]{:S(2)}) copy-start(f32[1024]{0:T(1024)} %param.15) | copy-start | bytes 12292
  471.1 39.9 %copy-start.4 = (f32[1,1024]{1,0:T(1,128)S(1)}, f32[1,1024]{1,0:T(1,128)}, u32[]{:S(2)}) copy-start(f32[1,1024]{1,0:T(1,128)} %get-tuple-element.11) | copy-start | bytes 12292
  471.1 39.9 %copy-start.5 = (f32[1,1024]{1,0:T(1,128)S(1)}, f32[1,1024]{1,0:T(1,128)}, u32[]{:S(2)}) copy-start(f32[1,1024]{1,0:T(1,128)} %get-tuple-element.12) | copy-start | bytes 12292
  471.1 39.9 %copy-start.6 = (f32[1,1024]{1,0:T(1,128)S(1)}, f32[1,1024]{1,0:T(1,128)}, u32[]{:S(2)}) copy-start(f32[1,1024]{1,0:T(1,128)} %get-tuple-element.13) | copy-start | bytes 12292
  471.1 39.9 %copy-start.7 = (f32[1,1024]{1,0:T(1,128)S(1)}, f32[1,1024]{1,0:T(1,128)}, u32[]{:S(2)}) copy-start(f32[1,1024]{1,0:T(1,128)} %get-tuple-element.14) | copy-start | bytes 12292
  471.1 39.9 %copy-start.8 = (f32[1,1024]{1,0:T(1,128)S(1)}, f32[1,1024]{1,0:T(1,128)}, u32[]{:S(2)}) copy-start(f32[1,1024]{1,0:T(1,128)} %get-tuple-element.15) | copy-start | bytes 12292
  471.1 39.9 %copy-start.9 = (f32[1,1024]{1,0:T(1,128)S(1)}, f32[1,1024]{1,0:T(1,128)}, u32[]{:S(2)}) copy-start(f32[1,1024]{1,0:T(1,128)} %get-tuple-element.16) | copy-start | bytes 12292
  471.1 39.9 %copy-start.10 = (f32[1,1024]{1,0:T(1,128)S(1)}, f32[1,1024]{1,0:T(1,128)}, u32[]{:S(2)}) copy-start(f32[1,1024]{1,0:T(1,128)} %get-tuple-element.17) | copy-start | bytes 12292
  471.1 39.9 %copy-start.11 = (f32[1,1024]{1,0:T(1,128)S(1)}, f32[1,1024]{1,0:T(1,128)}, u32[]{:S(2)}) copy-start(f32[1,1024]{1,0:T(1,128)} %get-tuple-element.18) | copy-start | bytes 12292
  471.1 39.9 %copy-start.12 = (f32[1,1024]{1,0:T(1,128)S(1)}, f32[1,1024]{1,0:T(1,128)}, u32[]{:S(2)}) copy-start(f32[1,1024]{1,0:T(1,128)} %get-tuple-element.19) | copy-start | bytes 12292
  471.1 39.9 %copy-start.13 = (f32[1,1024]{1,0:T(1,128)S(1)}, f32[1,1024]{1,0:T(1,128)}, u32[]{:S(2)}) copy-start(f32[1,1024]{1,0:T(1,128)} %get-tuple-element.20) | copy-start | bytes 12292
  471.2 39.9 %copy-start.14 = (f32[1,1024]{1,0:T(1,128)S(1)}, f32[1,1024]{1,0:T(1,128)}, u32[]{:S(2)}) copy-start(f32[1,1024]{1,0:T(1,128)} %get-tuple-element.21) | copy-start | bytes 12292
  471.2 39.9 %copy-start.15 = (f32[1,1024]{1,0:T(1,128)S(1)}, f32[1,1024]{1,0:T(1,128)}, u32[]{:S(2)}) copy-start(f32[1,1024]{1,0:T(1,128)} %get-tuple-element.22) | copy-start | bytes 12292
  471.2 39.9 %copy-start.16 = (f32[1,1024]{1,0:T(1,128)S(1)}, f32[1,1024]{1,0:T(1,128)}, u32[]{:S(2)}) copy-start(f32[1,1024]{1,0:T(1,128)} %get-tuple-element.23) | copy-start | bytes 12292
  471.2 39.9 %copy-start.17 = (f32[1,1024]{1,0:T(1,128)S(1)}, f32[1,1024]{1,0:T(1,128)}, u32[]{:S(2)}) copy-start(f32[1,1024]{1,0:T(1,128)} %get-tuple-element.24) | copy-start | bytes 12292
  471.2 39.9 %copy-start.18 = (f32[1,1024]{1,0:T(1,128)S(1)}, f32[1,1024]{1,0:T(1,128)}, u32[]{:S(2)}) copy-start(f32[1,1024]{1,0:T(1,128)} %get-tuple-element.25) | copy-start | bytes 12292
  502.0 8.8 %collective-permute-start.1 = (f32[15,1024]{1,0:T(8,128)S(1)}, f32[15,1024]{1,0:T(8,128)S(1)}, u32[]{:S(2)}, u32[]{:S(2)}) collective-permute-start(f32[15,1024]{1,0:T(8,128)S(1)} %get-tuple-element.6), channel_id=1, source_target_pairs={{1,0},{2,1},{3,2},{4,3},{5,4},{6,5},{7,6},{8,7},{9,8},{10,9},{11,1... | collective-permute-start | bytes 184328 | tf_op jit(solution)/shard_map/ppermute | solution.py:18
  507.7 3.2 collective-permute-start
Sparse Core Ops, SparseCore 0:
  34.3 251.2 all-gather.1
